TPU v7x, 32 devices: a whole 2x2x4 slice. The times are simulated.
32 devices in a mesh: dp: 8 (over y, x, core), tensor: 4 (over z).
Axes of the slice: x: 2, y: 2, z: 4, core: 2. Of those that a mesh axis runs over, the one named last changes fastest.
Arguments:
- inputs: bfloat16 [2048, 1792], P('dp', 'tensor'), may hold values from -6 to 6
- cotangent: bfloat16 [2048, 1792], P('dp', 'tensor'), may hold values from -6 to 6
- documents: int32 [2048], P('dp'), may hold values from -1 to 3, as said below
- gains: bfloat16 [2, 1792], P(None, 'tensor'), may hold values from 0.5 to 1.5
- query_key: bfloat16 [1792, 2, 256], P(None, None, 'tensor'), may hold values from -0.125 to 0.125
- value_gate: bfloat16 [1792, 2, 1792], P(None, None, 'tensor'), may hold values from -0.125 to 0.125
- conv_taps: bfloat16 [4, 1792], P(None, 'tensor'), may hold values from -3 to 3
- output_weight: bfloat16 [1792, 1792], P('tensor'), may hold values from -3 to 3
- gate_up: bfloat16 [1792, 2, 4096], P(None, None, 'tensor'), may hold values from -0.125 to 0.125
- down_weight: bfloat16 [4096, 1792], P('tensor'), may hold values from -0.09375 to 0.09375
- gains_moment: float32 [2, 1792], P(None, 'tensor'), may hold values from -60 to 60
- query_key_moment: float32 [1792, 2, 256], P('dp', None, 'tensor'), may hold values from -60 to 60
- value_gate_moment: float32 [1792, 2, 1792], P('dp', None, 'tensor'), may hold values from -60 to 60
- conv_taps_moment: float32 [4, 1792], P(None, 'tensor'), may hold values from -60 to 60
- output_weight_moment: float32 [1792, 1792], P('tensor', 'dp'), may hold values from -60 to 60
- gate_up_moment: float32 [1792, 2, 4096], P('dp', None, 'tensor'), may hold values from -60 to 60
- down_weight_moment: float32 [4096, 1792], P('tensor', 'dp'), may hold values from -60 to 60
- gains_mean: float32 [2, 1792], P(None, 'tensor'), may hold values from -4 to 4
- probe_lookup_smoothed: float32 [1792, 2, 256], P('dp', None, 'tensor'), may hold values from -0.125 to 0.125
- value_gate_mean: float32 [1792, 2, 1792], P('dp', None, 'tensor'), may hold values from -0.125 to 0.125
- conv_taps_mean: float32 [4, 1792], P(None, 'tensor'), may hold values from -3 to 3
- output_weight_mean: float32 [1792, 1792], P('tensor', 'dp'), may hold values from -3 to 3
- gate_up_mean: float32 [1792, 2, 4096], P('dp', None, 'tensor'), may hold values from -0.125 to 0.125
- down_weight_mean: float32 [4096, 1792], P('tensor', 'dp'), may hold values from -0.09375 to 0.09375
Outputs:
- mixed: bfloat16 [2048, 1792], P('dp', 'tensor')
- input_grad: float32 [2048, 1792], P('dp', 'tensor')
- gains_grad: float32 [2, 1792], P(None, 'tensor')
- query_key_grad: float32 [1792, 2, 256], P('dp', None, 'tensor')
- value_gate_grad: float32 [1792, 2, 1792], P('dp', None, 'tensor')
- conv_taps_grad: float32 [4, 1792], P(None, 'tensor')
- output_weight_grad: float32 [1792, 1792], P('tensor', 'dp')
- gate_up_grad: float32 [1792, 2, 4096], P('dp', None, 'tensor')
- down_weight_grad: float32 [4096, 1792], P('tensor', 'dp')
- gains_change: float32 [2, 1792], P(None, 'tensor')
- query_key_change: float32 [1792, 2, 256], P('dp', None, 'tensor')
- value_gate_change: float32 [1792, 2, 1792], P('dp', None, 'tensor')
- conv_taps_change: float32 [4, 1792], P(None, 'tensor')
- output_weight_change: float32 [1792, 1792], P('tensor', 'dp')
- gate_up_change: float32 [1792, 2, 4096], P('dp', None, 'tensor')
- down_weight_change: float32 [4096, 1792], P('tensor', 'dp')
- gains_momentum: float32 [2, 1792], P(None, 'tensor')
- query_key_momentum: float32 [1792, 2, 256], P('dp', None, 'tensor')
- value_gate_momentum: float32 [1792, 2, 1792], P('dp', None, 'tensor')
- conv_taps_momentum: float32 [4, 1792], P(None, 'tensor')
- output_weight_momentum: float32 [1792, 1792], P('tensor', 'dp')
- gate_up_momentum: float32 [1792, 2, 4096], P('dp', None, 'tensor')
- down_weight_momentum: float32 [4096, 1792], P('tensor', 'dp')
- gains_average: float32 [2, 1792], P(None, 'tensor')
- query_key_average: float32 [1792, 2, 256], P('dp', None, 'tensor')
- value_gate_average: float32 [1792, 2, 1792], P('dp', None, 'tensor')
- conv_taps_average: float32 [4, 1792], P(None, 'tensor')
- output_weight_average: float32 [1792, 1792], P('tensor', 'dp')
- gate_up_average: float32 [1792, 2, 4096], P('dp', None, 'tensor')
- down_weight_average: float32 [4096, 1792], P('tensor', 'dp')
Inputs may be any that keep to these rules, and one draw needn't show every extreme that they name: `documents`: within each aligned block of 256 rows the numbers start at 0 and never fall; a document spans at least 64 and at most 256 rows (the last one before padding may be shorter), and the first block holds a single document; each block ends with at least one and fewer than 64 padding rows marked -1, and has no other -1.
All inputs are finite; a program needn't handle non-finite values.
Results may differ from a plain program's by a relative error of at most 0.013.
Values may be sent and summed in bfloat16 or wider, within the bound.
No kernel may reach another device: no remote copies, remote signals or barrier semaphores. Data moves between devices by JAX's collectives and lax.ppermute only.
A program may use at most 192 MiB of HBM per device.

v0:
```python
import math
import jax
import jax.numpy as jnp
from jax import lax
from jax.sharding import PartitionSpec as P

H = 16
F = 16
KERNEL = 4
BLOCK = 256
epsilon = 1e-06
momentum_decay = 0.9
learning_rate = 0.001
average_rate = 0.1


def silu_slope(argument):
    logistic_output = jax.nn.sigmoid(argument)
    return logistic_output * (1.0 + argument * (1.0 - logistic_output))


def shift_down(source, offset, filler):
    pad_width = [(offset, 0)] + [(0, 0)] * (source.ndim - 1)
    return jnp.pad(source, pad_width, constant_values=filler)[: source.shape[0]]


def shift_up(source, offset, filler):
    pad_width = [(0, offset)] + [(0, 0)] * (source.ndim - 1)
    return jnp.pad(source, pad_width, constant_values=filler)[offset:]


def convolve(values_pre, tap_weights, documents):
    summed = values_pre * tap_weights[0]
    for offset in range(1, KERNEL):
        same_doc = (shift_down(documents, offset, -2) == documents)[:, None]
        summed = summed + jnp.where(
            same_doc, shift_down(values_pre, offset, 0.0) * tap_weights[offset], 0.0
        )
    return summed


def advance(grad, weight, moment, average):
    moment_new = momentum_decay * moment + (1.0 - momentum_decay) * grad
    change = -learning_rate * ((1.0 - momentum_decay) * grad + momentum_decay * moment_new)
    average_new = average + average_rate * (weight.astype(jnp.float32) + change - average)
    return (change, moment_new, average_new)


def local(
    inputs,
    cotangent,
    documents,
    gains,
    query_key,
    value_gate,
    conv_taps,
    output_weight,
    gate_up,
    down_weight,
    gains_moment,
    query_key_moment,
    value_gate_moment,
    conv_taps_moment,
    output_weight_moment,
    gate_up_moment,
    down_weight_moment,
    gains_mean,
    probe_lookup_smoothed,
    value_gate_mean,
    conv_taps_mean,
    output_weight_mean,
    gate_up_mean,
    down_weight_mean,
):
    tokens = inputs.shape[0]
    feature_share = inputs.shape[1]
    groups = lax.axis_size("tensor")
    model_width = feature_share * groups
    local_heads = H // groups
    head_size = model_width // H
    score_factor_scale = 1.0 / math.sqrt(F)
    own_start = lax.axis_index("tensor") * feature_share

    def own_columns(source):
        return lax.dynamic_slice_in_dim(source, own_start, feature_share, source.ndim - 1)

    whole_inputs, whole_gains = (
        lax.all_gather(inputs, "tensor", axis=1, tiled=True),
        lax.all_gather(gains, "tensor", axis=1, tiled=True),
    )
    inputs_wide = whole_inputs.astype(jnp.float32)
    gain_one = whole_gains[0].astype(jnp.float32)
    gain_two = whole_gains[1].astype(jnp.float32)
    root_one = lax.rsqrt(jnp.mean(inputs_wide * inputs_wide, axis=1, keepdims=True) + epsilon)
    unit_one = inputs_wide * root_one
    normed = (unit_one * gain_one).astype(jnp.bfloat16)
    projected = jnp.einsum(
        "td,dsf->tsf", normed, query_key, preferred_element_type=jnp.float32
    ).astype(jnp.bfloat16)
    queries = projected[:, 0].reshape(tokens, local_heads, F)
    keys = projected[:, 1].reshape(tokens, local_heads, F)
    mixing = jnp.einsum("td,dsf->tsf", normed, value_gate, preferred_element_type=jnp.float32)
    values_pre = mixing[:, 0]
    gates = mixing[:, 1]
    tap_weights = conv_taps.astype(jnp.float32)
    mixed_values = (
        convolve(values_pre, tap_weights, documents)
        .astype(jnp.bfloat16)
        .reshape(tokens, local_heads, head_size)
    )
    margin = 2 * BLOCK
    key_pad = jnp.pad(keys, ((margin, 0), (0, 0), (0, 0)))
    value_pad = jnp.pad(mixed_values, ((margin, 0), (0, 0), (0, 0)))
    docs_pad = jnp.pad(documents, (margin, 0), constant_values=-2)
    block_count = tokens // BLOCK

    def window(block_index):
        first = block_index * BLOCK
        row_index = first + jnp.arange(BLOCK, dtype=jnp.int32)
        column_index = first - margin + jnp.arange(3 * BLOCK, dtype=jnp.int32)
        allowed = (documents[:, None] == docs_pad[None, :]) & (
            column_index[None, :] <= row_index[:, None]
        )
        attention_scores = (
            jnp.einsum("cyg,jyg->ycj", queries, key_pad, preferred_element_type=jnp.float32)
            * score_factor_scale
        )
        weights = jnp.where(
            allowed[None], 1.0 + attention_scores + 0.5 * attention_scores * attention_scores, 0.0
        )
        return (queries, key_pad, value_pad, allowed, attention_scores, weights)

    def forward_block(block_index):
        query_matrix_rows, lookup_lines_array, value_rows, allowed, attention_scores, weights = (
            window(block_index)
        )
        totals = jnp.sum(weights, axis=2)
        probs = (weights / totals[:, :, None]).astype(jnp.bfloat16)
        result = jnp.einsum("hqk,khe->qhe", probs, value_rows, preferred_element_type=jnp.float32)
        return (result, totals)

    attended, kept_totals = lax.map(forward_block, jnp.arange(block_count, dtype=jnp.int32))
    attended = attended.reshape(tokens, feature_share)
    gate_silu = jax.nn.silu(gates)
    gated = (attended * gate_silu).astype(jnp.bfloat16)
    branch = lax.psum(jnp.dot(gated, output_weight, preferred_element_type=jnp.float32), "tensor")
    hidden = inputs_wide + branch
    root_two = lax.rsqrt(jnp.mean(hidden * hidden, axis=1, keepdims=True) + epsilon)
    unit_two = hidden * root_two
    normed_two = (unit_two * gain_two).astype(jnp.bfloat16)
    inner = jnp.einsum("td,dsf->tsf", normed_two, gate_up, preferred_element_type=jnp.float32)
    opener_before_squash = inner[:, 0]
    up_pre = inner[:, 1]
    unit_silu = jax.nn.silu(opener_before_squash)
    activation = (unit_silu * up_pre).astype(jnp.bfloat16)
    feed = lax.psum_scatter(
        jnp.dot(activation, down_weight, preferred_element_type=jnp.float32).astype(jnp.bfloat16),
        "tensor",
        scatter_dimension=1,
        tiled=True,
    ).astype(jnp.float32)
    mixed = (own_columns(hidden) + feed).astype(jnp.bfloat16)
    masked = jnp.where(documents[:, None] >= 0, cotangent, jnp.zeros_like(cotangent))
    cot_whole = lax.all_gather(masked, "tensor", axis=1, tiled=True)
    down_local = jnp.einsum("tf,td->fd", activation, cot_whole, preferred_element_type=jnp.float32)
    d_act = jnp.einsum("td,fd->tf", cot_whole, down_weight, preferred_element_type=jnp.float32)
    d_inner = jnp.stack(
        [d_act * up_pre * silu_slope(opener_before_squash), d_act * unit_silu], axis=1
    ).astype(jnp.bfloat16)
    gate_up_local = jnp.einsum(
        "td,tsf->dsf", normed_two, d_inner, preferred_element_type=jnp.float32
    )
    d_normed_two = lax.psum(
        jnp.einsum("tsf,dsf->td", d_inner, gate_up, preferred_element_type=jnp.float32), "tensor"
    )
    scaled_two = d_normed_two * gain_two
    gain_two_grad = jnp.sum(d_normed_two * unit_two, axis=0)
    d_hidden = cot_whole.astype(jnp.float32) + root_two * (
        scaled_two - unit_two * jnp.mean(scaled_two * unit_two, axis=1, keepdims=True)
    )
    d_branch = d_hidden.astype(jnp.bfloat16)
    output_local = jnp.einsum("tc,td->cd", gated, d_branch, preferred_element_type=jnp.float32)
    d_gated = jnp.einsum("td,cd->tc", d_branch, output_weight, preferred_element_type=jnp.float32)
    d_attended = (d_gated * gate_silu).astype(jnp.bfloat16).reshape(tokens, local_heads, head_size)
    d_gates = (d_gated * attended * silu_slope(gates)).astype(jnp.bfloat16)

    def backward_block(carry, block_index):
        key_acc, payload_accumulator = carry
        query_matrix_rows, lookup_lines_array, value_rows, allowed, attention_scores, weights = (
            window(block_index)
        )
        totals = kept_totals[block_index]
        probs = weights / totals[:, :, None]
        first = block_index * BLOCK
        value_part = jnp.einsum(
            "hqk,qhe->khe",
            probs.astype(jnp.bfloat16),
            d_attended,
            preferred_element_type=jnp.float32,
        )
        d_probs = jnp.einsum(
            "qhe,khe->hqk", d_attended, value_rows, preferred_element_type=jnp.float32
        )
        d_weights = (d_probs - jnp.sum(d_probs * probs, axis=2, keepdims=True)) / totals[:, :, None]
        logit_slope_delta = jnp.where(
            allowed[None], d_weights * (1.0 + attention_scores), 0.0
        ).astype(jnp.bfloat16)
        query_part = (
            jnp.einsum(
                "ogw,wox->gox",
                logit_slope_delta,
                lookup_lines_array,
                preferred_element_type=jnp.float32,
            )
            * score_factor_scale
        )
        key_part = (
            jnp.einsum(
                "naj,ano->jno",
                logit_slope_delta,
                query_matrix_rows,
                preferred_element_type=jnp.float32,
            )
            * score_factor_scale
        )
        key_acc = key_acc + key_part
        payload_accumulator = payload_accumulator + value_part
        return ((key_acc, payload_accumulator), query_part)

    start_carry = (
        jnp.zeros((tokens + margin, local_heads, F), jnp.float32),
        jnp.zeros((tokens + margin, local_heads, head_size), jnp.float32),
    )
    (key_acc, payload_accumulator), query_parts = lax.scan(
        backward_block, start_carry, jnp.arange(block_count, dtype=jnp.int32)
    )
    d_queries = query_parts.reshape(tokens, local_heads * F).astype(jnp.bfloat16)
    d_keys = key_acc[margin:].reshape(tokens, local_heads * F).astype(jnp.bfloat16)
    d_mixed = payload_accumulator[margin:].reshape(tokens, feature_share)
    d_values = d_mixed * tap_weights[0]
    tap_rows = [jnp.sum(d_mixed * values_pre, axis=0)]
    for offset in range(1, KERNEL):
        same_doc = (shift_down(documents, offset, -2) == documents)[:, None]
        masked_grad = jnp.where(same_doc, d_mixed, 0.0)
        d_values = d_values + shift_up(masked_grad, offset, 0.0) * tap_weights[offset]
        tap_rows.append(jnp.sum(masked_grad * shift_down(values_pre, offset, 0.0), axis=0))
    conv_local = jnp.stack(tap_rows)
    d_query_key = jnp.stack([d_queries, d_keys], axis=1)
    delta_worth_opener = jnp.stack([d_values.astype(jnp.bfloat16), d_gates], axis=1)
    query_key_local = jnp.einsum(
        "td,tsf->dsf", normed, d_query_key, preferred_element_type=jnp.float32
    )
    value_gate_local = jnp.einsum(
        "td,tsf->dsf", normed, delta_worth_opener, preferred_element_type=jnp.float32
    )
    d_normed_part = jnp.einsum(
        "tsf,dsf->td", d_query_key, query_key, preferred_element_type=jnp.float32
    )
    d_normed_part = d_normed_part + jnp.einsum(
        "tsf,dsf->td", delta_worth_opener, value_gate, preferred_element_type=jnp.float32
    )
    d_normed = lax.psum(d_normed_part, "tensor")
    scaled_one = d_normed * gain_one
    full_grad = d_hidden + root_one * (
        scaled_one - unit_one * jnp.mean(scaled_one * unit_one, axis=1, keepdims=True)
    )
    input_grad = own_columns(full_grad)
    gain_one_grad = own_columns(jnp.sum(d_normed * unit_one, axis=0))
    gains_local = jnp.stack([gain_one_grad, own_columns(gain_two_grad)])
    gains_grad, conv_taps_grad = lax.psum((gains_local, conv_local), "dp")
    query_key_grad, value_gate_grad, gate_up_grad, output_weight_grad, down_weight_grad = (
        lax.psum_scatter(query_key_local, "dp", scatter_dimension=0, tiled=True),
        lax.psum_scatter(value_gate_local, "dp", scatter_dimension=0, tiled=True),
        lax.psum_scatter(gate_up_local, "dp", scatter_dimension=0, tiled=True),
        lax.psum_scatter(output_local, "dp", scatter_dimension=1, tiled=True),
        lax.psum_scatter(down_local, "dp", scatter_dimension=1, tiled=True),
    )
    dp_index = lax.axis_index("dp")
    dp_count = lax.axis_size("dp")

    def own_rows(source, axis_dim):
        length = source.shape[axis_dim] // dp_count
        return lax.dynamic_slice_in_dim(source, dp_index * length, length, axis_dim)

    gains_change, gains_momentum, gains_average = advance(
        gains_grad, gains, gains_moment, gains_mean
    )
    query_key_change, query_key_momentum, query_key_average = advance(
        query_key_grad, own_rows(query_key, 0), query_key_moment, probe_lookup_smoothed
    )
    value_gate_change, value_gate_momentum, value_gate_average = advance(
        value_gate_grad, own_rows(value_gate, 0), value_gate_moment, value_gate_mean
    )
    conv_taps_change, conv_taps_momentum, conv_taps_average = advance(
        conv_taps_grad, conv_taps, conv_taps_moment, conv_taps_mean
    )
    output_weight_change, output_weight_momentum, output_weight_average = advance(
        output_weight_grad, own_rows(output_weight, 1), output_weight_moment, output_weight_mean
    )
    gate_up_change, gate_up_momentum, gate_up_average = advance(
        gate_up_grad, own_rows(gate_up, 0), gate_up_moment, gate_up_mean
    )
    down_weight_change, down_weight_momentum, down_weight_average = advance(
        down_weight_grad, own_rows(down_weight, 1), down_weight_moment, down_weight_mean
    )
    return (
        mixed,
        input_grad,
        gains_grad,
        query_key_grad,
        value_gate_grad,
        conv_taps_grad,
        output_weight_grad,
        gate_up_grad,
        down_weight_grad,
        gains_change,
        query_key_change,
        value_gate_change,
        conv_taps_change,
        output_weight_change,
        gate_up_change,
        down_weight_change,
        gains_momentum,
        query_key_momentum,
        value_gate_momentum,
        conv_taps_momentum,
        output_weight_momentum,
        gate_up_momentum,
        down_weight_momentum,
        gains_average,
        query_key_average,
        value_gate_average,
        conv_taps_average,
        output_weight_average,
        gate_up_average,
        down_weight_average,
    )


def solution(mesh):
    return jax.shard_map(
        local,
        mesh=mesh,
        in_specs=(
            P("dp", "tensor"),
            P("dp", "tensor"),
            P("dp"),
            P(None, "tensor"),
            P(None, None, "tensor"),
            P(None, None, "tensor"),
            P(None, "tensor"),
            P("tensor", None),
            P(None, None, "tensor"),
            P("tensor", None),
            P(None, "tensor"),
            P("dp", None, "tensor"),
            P("dp", None, "tensor"),
            P(None, "tensor"),
            P("tensor", "dp"),
            P("dp", None, "tensor"),
            P("tensor", "dp"),
            P(None, "tensor"),
            P("dp", None, "tensor"),
            P("dp", None, "tensor"),
            P(None, "tensor"),
            P("tensor", "dp"),
            P("dp", None, "tensor"),
            P("tensor", "dp"),
        ),
        out_specs=(
            P("dp", "tensor"),
            P("dp", "tensor"),
            P(None, "tensor"),
            P("dp", None, "tensor"),
            P("dp", None, "tensor"),
            P(None, "tensor"),
            P("tensor", "dp"),
            P("dp", None, "tensor"),
            P("tensor", "dp"),
            P(None, "tensor"),
            P("dp", None, "tensor"),
            P("dp", None, "tensor"),
            P(None, "tensor"),
            P("tensor", "dp"),
            P("dp", None, "tensor"),
            P("tensor", "dp"),
            P(None, "tensor"),
            P("dp", None, "tensor"),
            P("dp", None, "tensor"),
            P(None, "tensor"),
            P("tensor", "dp"),
            P("dp", None, "tensor"),
            P("tensor", "dp"),
            P(None, "tensor"),
            P("dp", None, "tensor"),
            P("dp", None, "tensor"),
            P(None, "tensor"),
            P("tensor", "dp"),
            P("dp", None, "tensor"),
            P("tensor", "dp"),
        ),
        check_vma=False,
    )
```

profile of v0, /device:TPU:0, one launch (start us, length us, event | category | flops | bytes accessed | tf_op | source)
XLA Modules:
  0.0 709.4 jit_solution(10752097913392679788)
XLA Ops:
  7.3 23.5 %all_gather.9 = bf16[256,1792]{0,1:T(8,128)(2,1)} all-gather(bf16[256,448]{0,1:T(8,128)(2,1)} %param.24), channel_id=1, replica_groups=mesh['dp'=8,'tensor'=4] {'tensor'}, dimensions={1}, use_global_device_ids=true | all-gather | bytes 1146880 | tf_op jit(solution)/shard_map/all_gather | solution.py:88
  33.0 11.9 %all-gather = bf16[4,448,2]{1,2,0:T(2,128)(2,1)S(1)} all-gather(bf16[1,448,2]{1,2,0:T(2,128)(2,1)S(1)} %bitcast.173), channel_id=1, replica_groups=mesh['dp'=8,'tensor'=4] {'tensor'}, dimensions={0}, use_global_device_ids=true | all-gather | bytes 8960 | tf_op jit(solution)/shard_map/all_gather | solution.py:89
  57.5 29.3 %all_gather.11 = bf16[256,1792]{0,1:T(8,128)(2,1)} all-gather(bf16[256,448]{0,1:T(8,128)(2,1)S(1)} %broadcast_select_fusion), channel_id=1, replica_groups=mesh['dp'=8,'tensor'=4] {'tensor'}, dimensions={1}, use_global_device_ids=true | all-gather | bytes 1146880 | tf_op jit(solution)/shard_map/all_gather | solution.py:164
  86.8 56.6 %all-reduce.17.cloned.1.call-done = f32[256,1792]{1,0:T(8,128)} async-done(((f32[256,1792]{1,0:T(8,128)}), f32[256,1792]{1,0:T(8,128)}) %all-reduce.17.cloned.1.call-update) | async-done | bytes 1835024 | tf_op jit(solution)/shard_map/psum | solution.py:146
  145.7 6.3 fusion.53
  155.3 3.8 convolution_bitcast_fusion.3
  161.4 4.7 fusion.3
  166.3 69.5 %all-reduce.19.cloned.1.call-done = f32[256,1792]{1,0:T(8,128)} async-done(((f32[256,1792]{1,0:T(8,128)}), f32[256,1792]{1,0:T(8,128)}) %all-reduce.19.cloned.1.call-update) | async-done | bytes 1835024 | tf_op jit(solution)/shard_map/psum | solution.py:173
  235.9 3.3 multiply_reduce_fusion.1
  245.6 10.6 %fusion.11 = bf16[768,4,16]{0,2,1:T(8,128)(2,1)} fusion(bf16[256,4,16]{0,2,1:T(8,128)(2,1)S(1)} %bitcast.162, f32[4,256,768]{2,1,0:T(8,128)} %fusion.20, f32[4,256,768]{2,1,0:T(8,128)} %copy-done.47, f32[4,256]{1,0:T(4,128)S(1)} %get-tuple-element.236, pred[256,768]{1,0:T(8,128)(4,1)} %copy-done.28), kind=kOutput, calls=%fused_computation.33 | convolution fusion | flops 37062400 | bytes 6623232 | tf_op jit(solution)/shard_map/while/body/eval_jaxpr/naj,ano->jno/dot_general | solution.py:218
  256.9 10.2 %fusion.12 = bf16[4,16,256]{2,1,0:T(8,128)(2,1)S(1)} fusion(f32[4,256,768]{2,1,0:T(8,128)} %fusion.20, f32[4,256,768]{2,1,0:T(8,128)} %copy-done.47, f32[4,256]{1,0:T(4,128)S(1)} %get-tuple-element.236, pred[256,768]{1,0:T(8,128)(4,1)} %copy-done.28, bf16[256,4,16]{0,2,1:T(8,128)(2,1)} %bitcast.160), kind=kOutput, calls=%fused_computation.35 | convolution fusion | flops 36996864 | bytes 6557696 | tf_op jit(solution)/shard_map/while/body/eval_jaxpr/ogw,wox->gox/dot_general | solution.py:209
  267.2 2.7 fusion.74
  269.9 4.2 convolution_bitcast_fusion.4
  281.2 4.0 convolution_bitcast_fusion
  285.5 5.4 fusion.88
  291.9 5.4 fusion.15
  297.3 9.2 %fusion.27 = f32[1792,2,1024]{2,0,1:T(8,128)} fusion(bf16[256,1,1024]{2,0,1:T(8,128)(2,1)} %copy-done.23, bf16[256,1,1024]{2,0,1:T(8,128)(2,1)} %copy-done.22, f32[256,1792]{1,0:T(8,128)} %copy-done.1, f32[1792]{0:T(1024)S(1)} %get-tuple-element.184, f32[256]{0:T(256)S(1)} %add_rsqrt_fusion), kind=kOutput, calls=%fused_computation.71 | convolution fusion | flops 1882521600 | bytes 17571840 | tf_op jit(solution)/shard_map/td,tsf->dsf/dot_general | solution.py:170
  306.6 8.4 %copy.109 = bf16[1792,2,1024]{2,0,1:T(8,128)(2,1)} copy(bf16[1792,2,1024]{2,1,0:T(2,128)(2,1)} %param.32) | data formatting | bytes 14680064 | tf_op args[8]
  330.9 58.2 %all-reduce.21.cloned.1.call-done = f32[256,1792]{1,0:T(8,128)} async-done(((f32[256,1792]{1,0:T(8,128)}), f32[256,1792]{1,0:T(8,128)}) %all-reduce.21.cloned.1.call-update) | async-done | bytes 1835024 | tf_op jit(solution)/shard_map/psum | solution.py:262
  391.5 2.5 dynamic-slice_add_fusion
  396.0 23.6 %all-reduce.12 = (f32[2,448]{1,0:T(2,128)S(1)}, f32[4,448]{1,0:T(4,128)S(1)}) all-reduce(f32[2,448]{1,0:T(2,128)S(1)} %pad_maximum_fusion.8, f32[4,448]{1,0:T(4,128)S(1)} %pad_maximum_fusion.7), channel_id=1, replica_groups=mesh['dp'=8,'tensor'=4] {'dp'}, use_global_device_ids=true, to_apply=%region_12.13 | all-reduce | flops 2688 | bytes 21504 | tf_op jit(solution)/shard_map/psum | solution.py:270
  421.0 19.0 %reduce-scatter.23.cloned.1.call-done = f32[224,448]{1,0:T(8,128)} async-done(((f32[1792,448]{1,0:T(8,128)}), f32[224,448]{1,0:T(8,128)}) %reduce-scatter.23.cloned.1.call-update) | async-done | bytes 401424
  442.0 2.7 multiply_add_fusion.5
  444.7 66.3 %reduce-scatter.17.cloned.1.call-done = f32[1024,224]{0,1:T(8,128)} async-done(((f32[1024,1792]{0,1:T(8,128)}), f32[1024,224]{0,1:T(8,128)}) %reduce-scatter.17.cloned.1.call-update) | async-done | bytes 917520 | tf_op jit(solution)/shard_map/reduce_scatter | solution.py:276
  511.0 3.9 multiply_add_fusion.2
  514.8 66.4 %reduce-scatter.13.cloned.1.call-done = f32[224,2,448]{2,0,1:T(8,128)} async-done(((f32[1792,2,448]{2,0,1:T(8,128)}), f32[224,2,448]{2,0,1:T(8,128)}) %reduce-scatter.13.cloned.1.call-update) | async-done | bytes 802832 | tf_op jit(solution)/shard_map/reduce_scatter | solution.py:273
  590.3 96.9 %reduce-scatter.15.cloned.1.call-done = f32[224,2,1024]{2,0,1:T(8,128)} async-done(((f32[1792,2,1024]{2,0,1:T(8,128)}), f32[224,2,1024]{2,0,1:T(8,128)}) %reduce-scatter.15.cloned.1.call-update) | async-done | bytes 1835024 | tf_op jit(solution)/shard_map/reduce_scatter | solution.py:274
  687.2 4.6 multiply_add_fusion
  691.8 2.6 copy.129
  694.4 2.6 copy.131
  697.1 2.6 copy.133
  699.7 2.6 copy.127
  (183 shorter events, 70.5 us)
Async XLA Ops:
  7.2 39.3 %copy-start = (bf16[1792,2,448]{0,2,1:T(8,128)(2,1)S(1)}, bf16[1792,2,448]{0,2,1:T(8,128)(2,1)}, u32[]{:S(2)}) copy-start(bf16[1792,2,448]{0,2,1:T(8,128)(2,1)} %param.29) | copy-start | bytes 9633796
  7.2 25.8 %copy-start.36 = (bf16[2,448]{1,0:T(2,128)(2,1)S(1)}, bf16[2,448]{1,0:T(2,128)(2,1)}, u32[]{:S(2)}) copy-start(bf16[2,448]{1,0:T(2,128)(2,1)} %param.27) | copy-start | bytes 5380
  7.2 136.2 %all-reduce.17.cloned.1.call-start = ((), (), s32[]{:S(2)}) async-start(), calls=%async_computation.6 | async-start | bytes 3670016 | tf_op jit(solution)/shard_map/psum | solution.py:146
  46.5 3.4 copy-start.30
  46.6 3.4 copy-start.32
  46.6 3.5 copy-start.3
  46.6 3.5 copy-start.20
  49.0 4.8 copy-start.17
  56.5 179.4 %all-reduce.19.cloned.1.call-start = ((), (), s32[]{:S(2)}) async-start(), calls=%async_computation.7 | async-start | bytes 3670016 | tf_op jit(solution)/shard_map/psum | solution.py:173
  143.4 11.9 %slice-start = ((s8[7340032]{0:T(1024)(128)(4,1)}), s8[4194304]{0:T(1024)(128)(4,1)S(1)}, s32[]{:S(2)}) async-start(s8[7340032]{0:T(1024)(128)(4,1)} %bitcast.136), calls=%async_computation.15 | async-start | bytes 8388608
  145.6 6.4 copy-start.1
  145.6 6.4 copy-start.4
  145.6 6.4 copy-start.29
  145.7 9.6 %slice-start.1 = ((s8[7340032]{0:T(1024)(128)(4,1)}), s8[3145728]{0:T(1024)(128)(4,1)S(1)}, s32[]{:S(2)}) async-start(s8[7340032]{0:T(1024)(128)(4,1)} %bitcast.136), calls=%async_computation.16 | async-start | bytes 6291456
  159.1 163.1 %reduce-scatter.19.cloned.1.call-start = ((), (), s32[]{:S(2)}) async-start(), calls=%async_computation.12 | async-start | bytes 1146880
  166.1 161.9 %reduce-scatter.21.cloned.1.call-start = ((), (), s32[]{:S(2)}) async-start(), calls=%async_computation.13 | async-start | bytes 1032192
  274.1 115.0 %all-reduce.21.cloned.1.call-start = ((), (), s32[]{:S(2)}) async-start(), calls=%async_computation.8 | async-start | bytes 3670016 | tf_op jit(solution)/shard_map/psum | solution.py:262
  281.1 158.9 %reduce-scatter.23.cloned.1.call-start = ((), (), s32[]{:S(2)}) async-start(), calls=%async_computation.14 | async-start | bytes 4128768
  285.3 225.7 %reduce-scatter.17.cloned.1.call-start = ((), (), s32[]{:S(2)}) async-start(), calls=%async_computation.11 | async-start | bytes 8257536 | tf_op jit(solution)/shard_map/reduce_scatter | solution.py:276
  290.9 290.3 %reduce-scatter.13.cloned.1.call-start = ((), (), s32[]{:S(2)}) async-start(), calls=%async_computation.9 | async-start | bytes 8257536 | tf_op jit(solution)/shard_map/reduce_scatter | solution.py:273
  297.3 389.9 %reduce-scatter.15.cloned.1.call-start = ((), (), s32[]{:S(2)}) async-start(), calls=%async_computation.10 | async-start | bytes 16515072 | tf_op jit(solution)/shard_map/reduce_scatter | solution.py:274
  318.0 9.9 %copy-start.38 = (f32[448]{0:T(512)S(1)}, f32[448]{0:T(512)}, u32[]{:S(2)}) copy-start(f32[448]{0:T(512)} %get-tuple-element.181) | copy-start | bytes 5380
  318.0 9.9 %copy-start.39 = (f32[448]{0:T(512)S(1)}, f32[448]{0:T(512)}, u32[]{:S(2)}) copy-start(f32[448]{0:T(512)} %get-tuple-element.182) | copy-start | bytes 5380
  318.0 9.9 %copy-start.40 = (f32[448]{0:T(512)S(1)}, f32[448]{0:T(512)}, u32[]{:S(2)}) copy-start(f32[448]{0:T(512)} %get-tuple-element.183) | copy-start | bytes 5380
  329.0 62.4 %copy-start.24 = (f32[224,128]{0,1:T(8,128)}, f32[224,128]{0,1:T(8,128)S(1)}, u32[]{:S(2)}) copy-start(f32[224,128]{0,1:T(8,128)S(1)} %copy.145) | copy-start | bytes 344068
  391.4 28.3 %copy-start.37 = (bf16[2,448]{1,0:T(2,128)(2,1)S(1)}, bf16[2,448]{1,0:T(2,128)(2,1)}, u32[]{:S(2)}) copy-start(bf16[2,448]{1,0:T(2,128)(2,1)} %param.27) | copy-start | bytes 5380
  391.4 28.3 %copy-start.44 = (f32[2,448]{1,0:T(2,128)S(1)}, f32[2,448]{1,0:T(2,128)}, u32[]{:S(2)}) copy-start(f32[2,448]{1,0:T(2,128)} %param.41) | copy-start | bytes 10756
  391.5 28.3 %copy-start.45 = (f32[2,448]{1,0:T(2,128)S(1)}, f32[2,448]{1,0:T(2,128)}, u32[]{:S(2)}) copy-start(f32[2,448]{1,0:T(2,128)} %param.34) | copy-start | bytes 10756
  391.5 28.9 %copy-start.33 = (f32[4,448]{1,0:T(4,128)S(1)}, f32[4,448]{1,0:T(4,128)}, u32[]{:S(2)}) copy-start(f32[4,448]{1,0:T(4,128)} %param.44) | copy-start | bytes 21508
  391.5 28.9 %copy-start.34 = (f32[4,448]{1,0:T(4,128)S(1)}, f32[4,448]{1,0:T(4,128)}, u32[]{:S(2)}) copy-start(f32[4,448]{1,0:T(4,128)} %param.37) | copy-start | bytes 21508
  419.7 95.1 %copy-start.35 = (f32[4,448]{1,0:T(4,128)}, f32[4,448]{1,0:T(4,128)S(1)}, u32[]{:S(2)}) copy-start(f32[4,448]{1,0:T(4,128)S(1)} %get-tuple-element.187) | copy-start | bytes 21508
  419.7 95.1 %copy-start.46 = (f32[2,448]{1,0:T(2,128)}, f32[2,448]{1,0:T(2,128)S(1)}, u32[]{:S(2)}) copy-start(f32[2,448]{1,0:T(2,128)S(1)} %get-tuple-element.186) | copy-start | bytes 10756
  (27 other events, 49.1 us)
Sparse Core Ops, SparseCore 0:
  56.6 86.7 all-reduce.16
  159.3 76.5 all-reduce.18
  238.8 24.2 reduce-scatter.18
  274.2 34.3 reduce-scatter.20
  311.4 77.5 all-reduce.20
  392.4 47.5 reduce-scatter.22
  444.0 66.9 reduce-scatter.16
  514.3 66.8 reduce-scatter.12
  584.8 102.3 reduce-scatter.14
where the time goes:
time: 715 us; the launch traced here: 709 us
  waiting for transfers between devices  433 us (61%)
  blocking collectives  88.4 us (12%)
  matrix products  82.2 us (11%)
  local copies, waits for them, and re-layouts  51.1 us (7%)
  other arithmetic  38.7 us (5%)
  between operations  15 us (2%)
    reduce_scatter x1, waiting for transfers between devices, local(): lax.psum_scatter(gate_up_local, 'dp', scatter_dimension=0, tiled=True)  96.9 us
    psum x1, waiting for transfers between devices, local(): lax.psum(jnp.einsum('tsf,dsf->td', d_inner, gate_up, preferred_element_ty...  69.5 us
    reduce_scatter x1, waiting for transfers between devices, local(): lax.psum_scatter(value_gate_local, 'dp', scatter_dimension=0, tiled=True)  66.4 us
    reduce_scatter x1, waiting for transfers between devices, local(): lax.psum_scatter(down_local, 'dp', scatter_dimension=1, tiled=True)  66.3 us
    psum x1, waiting for transfers between devices, local(): d_normed = lax.psum(d_normed_part, 'tensor')  58.2 us
    psum x1, waiting for transfers between devices, local(): lax.psum(jnp.dot(gated, output_weight, preferred_element_type=jnp.float32...  56.6 us
    unnamed x117, local copies, waits for them, and re-layouts  40.9 us
    all_gather x1, blocking collectives, local(): cot_whole = lax.all_gather(masked, 'tensor', axis=1, tiled=True)  29.3 us
  transfers between devices with their start and end apart: 9, of which 7 were waited for; matrix products, arithmetic and copies ran while one was open for 18% of the time, Pallas kernels for 0%

commit v1 on v0

--- a/solution.py
+++ b/solution.py
@@ -170,9 +170,9 @@
     gate_up_local = jnp.einsum(
         "td,tsf->dsf", normed_two, d_inner, preferred_element_type=jnp.float32
     )
-    d_normed_two = lax.psum(
-        jnp.einsum("tsf,dsf->td", d_inner, gate_up, preferred_element_type=jnp.float32), "tensor"
-    )
+    content = jnp.einsum("tsf,dsf->td", d_inner, gate_up, preferred_element_type=jnp.float32)
+    high = lax.all_gather(content, "tensor")
+    d_normed_two = jnp.sum(high, axis=0)
     scaled_two = d_normed_two * gain_two
     gain_two_grad = jnp.sum(d_normed_two * unit_two, axis=0)
     d_hidden = cot_whole.astype(jnp.float32) + root_two * (

time: 715 us -> 762 us (1.066)
  waiting for transfers between devices: 433 us -> 475 us
    all_gather x0 -> x1, waiting for transfers between devices: none -> 118 us  [local(): high = lax.all_gather(content, 'tensor')]
    psum x1 -> x0, waiting for transfers between devices: 69.5 us -> none  [local(): lax.psum(jnp.einsum('tsf,dsf->td', d_inner, gate_up, preferred_element_ty...]
    reduce_scatter x1, waiting for transfers between devices: 66.3 us -> 8.04 us  [local(): lax.psum_scatter(down_local, 'dp', scatter_dimension=1, tiled=True)]
    unnamed x12, waiting for transfers between devices: 19.2 us -> 51.5 us
    psum x1, waiting for transfers between devices: 58.2 us -> 76.9 us  [local(): d_normed = lax.psum(d_normed_part, 'tensor')]
    unnamed x117 -> x115, local copies, waits for them, and re-layouts: 40.9 us -> 41.4 us
  transfers between devices with their start and end apart: 9 -> 9, of which waited for: 7 -> 8; matrix products, arithmetic and copies ran while one was open for 18% -> 17% of each run, Pallas kernels for 0% -> 0%
where the time goes in v1:
time: 762 us; the launch traced here: 756 us
  waiting for transfers between devices  475 us (62%)
  blocking collectives  87.3 us (11%)
  matrix products  83.8 us (11%)
  local copies, waits for them, and re-layouts  51.6 us (7%)
  other arithmetic  43 us (6%)
  between operations  14.7 us (2%)
    all_gather x1, waiting for transfers between devices, local(): high = lax.all_gather(content, 'tensor')  118 us
    reduce_scatter x1, waiting for transfers between devices, local(): lax.psum_scatter(gate_up_local, 'dp', scatter_dimension=0, tiled=True)  96.9 us
    psum x1, waiting for transfers between devices, local(): d_normed = lax.psum(d_normed_part, 'tensor')  76.9 us
    reduce_scatter x1, waiting for transfers between devices, local(): lax.psum_scatter(value_gate_local, 'dp', scatter_dimension=0, tiled=True)  65.7 us
    psum x1, waiting for transfers between devices, local(): lax.psum(jnp.dot(gated, output_weight, preferred_element_type=jnp.float32...  57.1 us
    unnamed x12, waiting for transfers between devices  51.5 us
    unnamed x115, local copies, waits for them, and re-layouts  41.4 us
    all_gather x1, blocking collectives, local(): cot_whole = lax.all_gather(masked, 'tensor', axis=1, tiled=True)  28.4 us
  transfers between devices with their start and end apart: 9, of which 8 were waited for; matrix products, arithmetic and copies ran while one was open for 17% of the time, Pallas kernels for 0%

profile of v1, /device:TPU:0, one launch (start us, length us, event | category | flops | bytes accessed | tf_op | source)
XLA Modules:
  0.0 756.1 jit_solution(7103852405914927571)
XLA Ops:
  8.3 23.4 %all_gather.15 = bf16[256,1792]{0,1:T(8,128)(2,1)} all-gather(bf16[256,448]{0,1:T(8,128)(2,1)} %param.24), channel_id=1, replica_groups=mesh['dp'=8,'tensor'=4] {'tensor'}, dimensions={1}, use_global_device_ids=true | all-gather | bytes 1146880 | tf_op jit(solution)/shard_map/all_gather | solution.py:88
  33.9 11.9 %all-gather.1 = bf16[4,448,2]{1,2,0:T(2,128)(2,1)S(1)} all-gather(bf16[1,448,2]{1,2,0:T(2,128)(2,1)S(1)} %bitcast.175), channel_id=1, replica_groups=mesh['dp'=8,'tensor'=4] {'tensor'}, dimensions={0}, use_global_device_ids=true | all-gather | bytes 8960 | tf_op jit(solution)/shard_map/all_gather | solution.py:89
  58.3 28.4 %all_gather.17 = bf16[256,1792]{0,1:T(8,128)(2,1)} all-gather(bf16[256,448]{0,1:T(8,128)(2,1)S(1)} %broadcast_select_fusion), channel_id=1, replica_groups=mesh['dp'=8,'tensor'=4] {'tensor'}, dimensions={1}, use_global_device_ids=true | all-gather | bytes 1146880 | tf_op jit(solution)/shard_map/all_gather | solution.py:164
  86.7 57.1 %all-reduce.16.cloned.1.call-done = f32[256,1792]{1,0:T(8,128)} async-done(((f32[256,1792]{1,0:T(8,128)}), f32[256,1792]{1,0:T(8,128)}) %all-reduce.16.cloned.1.call-update) | async-done | bytes 1835024 | tf_op jit(solution)/shard_map/psum | solution.py:146
  146.1 6.3 fusion.53
  155.7 3.8 convolution_bitcast_fusion.3
  159.6 4.7 fusion.3
  164.4 5.8 fusion.88
  172.7 118.5 %all-gather.4.cloned.1.call-done = f32[1024,1792]{1,0:T(8,128)} async-done(((f32[256,1792]{1,0:T(8,128)}), f32[1024,1792]{1,0:T(8,128)}) %all-gather.4.cloned.1.call-update) | async-done | bytes 7340048 | tf_op jit(solution)/shard_map/all_gather | solution.py:174
  291.2 5.0 reduce_sum.122
  296.2 3.3 multiply_reduce_fusion.1
  306.0 10.6 %fusion.11 = bf16[768,4,16]{0,2,1:T(8,128)(2,1)} fusion(bf16[256,4,16]{0,2,1:T(8,128)(2,1)S(1)} %bitcast.164, f32[4,256,768]{2,1,0:T(8,128)} %fusion.20, f32[4,256,768]{2,1,0:T(8,128)} %copy-done.46, f32[4,256]{1,0:T(4,128)S(1)} %get-tuple-element.236, pred[256,768]{1,0:T(8,128)(4,1)} %copy-done.27), kind=kOutput, calls=%fused_computation.33 | convolution fusion | flops 37062400 | bytes 6623232 | tf_op jit(solution)/shard_map/while/body/eval_jaxpr/naj,ano->jno/dot_general | solution.py:218
  317.4 10.2 %fusion.12 = bf16[4,16,256]{2,1,0:T(8,128)(2,1)S(1)} fusion(f32[4,256,768]{2,1,0:T(8,128)} %fusion.20, f32[4,256,768]{2,1,0:T(8,128)} %copy-done.46, f32[4,256]{1,0:T(4,128)S(1)} %get-tuple-element.236, pred[256,768]{1,0:T(8,128)(4,1)} %copy-done.27, bf16[256,4,16]{0,2,1:T(8,128)(2,1)} %bitcast.162), kind=kOutput, calls=%fused_computation.35 | convolution fusion | flops 36996864 | bytes 6557696 | tf_op jit(solution)/shard_map/while/body/eval_jaxpr/ogw,wox->gox/dot_general | solution.py:209
  327.6 2.9 fusion.74
  330.5 4.7 convolution_bitcast_fusion.4
  342.4 4.2 convolution_bitcast_fusion
  347.6 5.4 fusion.15
  353.1 9.3 %fusion.27 = f32[1792,2,1024]{2,0,1:T(8,128)} fusion(bf16[256,1,1024]{2,0,1:T(8,128)(2,1)} %copy-done.23, bf16[256,1,1024]{2,0,1:T(8,128)(2,1)} %copy-done.22, f32[256,1792]{1,0:T(8,128)} %copy-done.1, f32[1792]{0:T(1024)S(1)} %get-tuple-element.184, f32[256]{0:T(256)S(1)} %add_rsqrt_fusion), kind=kOutput, calls=%fused_computation.71 | convolution fusion | flops 1882521600 | bytes 17571840 | tf_op jit(solution)/shard_map/td,tsf->dsf/dot_general | solution.py:170
  362.4 8.5 %copy.109 = bf16[1792,2,1024]{2,0,1:T(8,128)(2,1)} copy(bf16[1792,2,1024]{2,1,0:T(2,128)(2,1)} %param.32) | data formatting | bytes 14680064 | tf_op args[8]
  379.2 8.0 %reduce-scatter.17.cloned.1.call-done = f32[1024,224]{0,1:T(8,128)} async-done(((f32[1024,1792]{0,1:T(8,128)}), f32[1024,224]{0,1:T(8,128)}) %reduce-scatter.17.cloned.1.call-update) | async-done | bytes 917520 | tf_op jit(solution)/shard_map/reduce_scatter | solution.py:276
  387.3 3.8 multiply_add_fusion.2
  392.0 34.3 %reduce-scatter.21.cloned.1.call-done = f32[224,128]{1,0:T(8,128)} async-done(((f32[1792,128]{1,0:T(8,128)}), f32[224,128]{1,0:T(8,128)}) %reduce-scatter.21.cloned.1.call-update) | async-done | bytes 114704
  429.8 76.9 %all-reduce.18.cloned.1.call-done = f32[256,1792]{1,0:T(8,128)} async-done(((f32[256,1792]{1,0:T(8,128)}), f32[256,1792]{1,0:T(8,128)}) %all-reduce.18.cloned.1.call-update) | async-done | bytes 1835024 | tf_op jit(solution)/shard_map/psum | solution.py:262
  509.2 2.9 dynamic-slice_add_fusion
  516.1 23.5 %all-reduce.12 = (f32[2,448]{1,0:T(2,128)S(1)}, f32[4,448]{1,0:T(4,128)S(1)}) all-reduce(f32[2,448]{1,0:T(2,128)S(1)} %pad_maximum_fusion.8, f32[4,448]{1,0:T(4,128)S(1)} %pad_maximum_fusion.7), channel_id=1, replica_groups=mesh['dp'=8,'tensor'=4] {'dp'}, use_global_device_ids=true, to_apply=%region_12.13 | all-reduce | flops 2688 | bytes 21504 | tf_op jit(solution)/shard_map/psum | solution.py:270
  540.9 17.0 %reduce-scatter.23.cloned.1.call-done = f32[224,448]{1,0:T(8,128)} async-done(((f32[1792,448]{1,0:T(8,128)}), f32[224,448]{1,0:T(8,128)}) %reduce-scatter.23.cloned.1.call-update) | async-done | bytes 401424
  559.9 2.7 multiply_add_fusion.5
  562.6 65.7 %reduce-scatter.13.cloned.1.call-done = f32[224,2,448]{2,0,1:T(8,128)} async-done(((f32[1792,2,448]{2,0,1:T(8,128)}), f32[224,2,448]{2,0,1:T(8,128)}) %reduce-scatter.13.cloned.1.call-update) | async-done | bytes 802832 | tf_op jit(solution)/shard_map/reduce_scatter | solution.py:273
  637.2 96.9 %reduce-scatter.15.cloned.1.call-done = f32[224,2,1024]{2,0,1:T(8,128)} async-done(((f32[1792,2,1024]{2,0,1:T(8,128)}), f32[224,2,1024]{2,0,1:T(8,128)}) %reduce-scatter.15.cloned.1.call-update) | async-done | bytes 1835024 | tf_op jit(solution)/shard_map/reduce_scatter | solution.py:274
  734.1 4.6 multiply_add_fusion
  738.8 2.6 copy.129
  746.7 2.6 copy.127
  (181 shorter events, 75.4 us)
Async XLA Ops:
  7.2 40.2 %copy-start = (bf16[1792,2,448]{0,2,1:T(8,128)(2,1)S(1)}, bf16[1792,2,448]{0,2,1:T(8,128)(2,1)}, u32[]{:S(2)}) copy-start(bf16[1792,2,448]{0,2,1:T(8,128)(2,1)} %param.29) | copy-start | bytes 9633796
  7.2 26.6 %copy-start.35 = (bf16[2,448]{1,0:T(2,128)(2,1)S(1)}, bf16[2,448]{1,0:T(2,128)(2,1)}, u32[]{:S(2)}) copy-start(bf16[2,448]{1,0:T(2,128)(2,1)} %param.27) | copy-start | bytes 5380
  7.2 136.6 %all-reduce.16.cloned.1.call-start = ((), (), s32[]{:S(2)}) async-start(), calls=%async_computation.6 | async-start | bytes 3670016 | tf_op jit(solution)/shard_map/psum | solution.py:146
  8.2 44.3 %copy-start.40 = (pred[256]{0:T(512)(128)(4,1)}, pred[256]{0:T(512)(128)(4,1)S(1)}, u32[]{:S(2)}) copy-start(pred[256]{0:T(512)(128)(4,1)S(1)} %get-tuple-element.233) | copy-start | bytes 772
  8.2 44.4 %copy-start.41 = (pred[256]{0:T(512)(128)(4,1)}, pred[256]{0:T(512)(128)(4,1)S(1)}, u32[]{:S(2)}) copy-start(pred[256]{0:T(512)(128)(4,1)S(1)} %get-tuple-element.234) | copy-start | bytes 772
  8.3 44.4 %copy-start.42 = (pred[256]{0:T(512)(128)(4,1)}, pred[256]{0:T(512)(128)(4,1)S(1)}, u32[]{:S(2)}) copy-start(pred[256]{0:T(512)(128)(4,1)S(1)} %get-tuple-element.235) | copy-start | bytes 772
  47.4 3.4 copy-start.3
  47.4 3.4 copy-start.20
  49.9 4.7 copy-start.17
  57.3 233.9 %all-gather.4.cloned.1.call-start = ((), (), s32[]{:S(2)}) async-start(), calls=%async_computation.11 | async-start | bytes 9175040 | tf_op jit(solution)/shard_map/all_gather | solution.py:174
  143.8 11.9 %slice-start = ((s8[7340032]{0:T(1024)(128)(4,1)}), s8[4194304]{0:T(1024)(128)(4,1)S(1)}, s32[]{:S(2)}) async-start(s8[7340032]{0:T(1024)(128)(4,1)} %bitcast.137), calls=%async_computation.15 | async-start | bytes 8388608
  146.0 6.4 copy-start.1
  146.1 6.4 copy-start.5
  146.1 6.4 copy-start.28
  146.1 9.6 %slice-start.1 = ((s8[7340032]{0:T(1024)(128)(4,1)}), s8[3145728]{0:T(1024)(128)(4,1)S(1)}, s32[]{:S(2)}) async-start(s8[7340032]{0:T(1024)(128)(4,1)} %bitcast.137), calls=%async_computation.16 | async-start | bytes 6291456
  159.6 218.5 %reduce-scatter.19.cloned.1.call-start = ((), (), s32[]{:S(2)}) async-start(), calls=%async_computation.12 | async-start | bytes 1146880
  164.3 222.9 %reduce-scatter.17.cloned.1.call-start = ((), (), s32[]{:S(2)}) async-start(), calls=%async_computation.10 | async-start | bytes 8257536 | tf_op jit(solution)/shard_map/reduce_scatter | solution.py:276
  170.2 256.1 %reduce-scatter.21.cloned.1.call-start = ((), (), s32[]{:S(2)}) async-start(), calls=%async_computation.13 | async-start | bytes 1032192
  335.3 171.5 %all-reduce.18.cloned.1.call-start = ((), (), s32[]{:S(2)}) async-start(), calls=%async_computation.7 | async-start | bytes 3670016 | tf_op jit(solution)/shard_map/psum | solution.py:262
  342.4 215.5 %reduce-scatter.23.cloned.1.call-start = ((), (), s32[]{:S(2)}) async-start(), calls=%async_computation.14 | async-start | bytes 4128768
  346.7 281.6 %reduce-scatter.13.cloned.1.call-start = ((), (), s32[]{:S(2)}) async-start(), calls=%async_computation.8 | async-start | bytes 8257536 | tf_op jit(solution)/shard_map/reduce_scatter | solution.py:273
  353.0 381.1 %reduce-scatter.15.cloned.1.call-start = ((), (), s32[]{:S(2)}) async-start(), calls=%async_computation.9 | async-start | bytes 16515072 | tf_op jit(solution)/shard_map/reduce_scatter | solution.py:274
  379.2 12.8 %copy-start.37 = (f32[448]{0:T(512)S(1)}, f32[448]{0:T(512)}, u32[]{:S(2)}) copy-start(f32[448]{0:T(512)} %get-tuple-element.181) | copy-start | bytes 5380
  379.2 12.8 %copy-start.38 = (f32[448]{0:T(512)S(1)}, f32[448]{0:T(512)}, u32[]{:S(2)}) copy-start(f32[448]{0:T(512)} %get-tuple-element.182) | copy-start | bytes 5380
  379.2 12.7 %copy-start.39 = (f32[448]{0:T(512)S(1)}, f32[448]{0:T(512)}, u32[]{:S(2)}) copy-start(f32[448]{0:T(512)} %get-tuple-element.183) | copy-start | bytes 5380
  509.1 30.5 %copy-start.36 = (bf16[2,448]{1,0:T(2,128)(2,1)S(1)}, bf16[2,448]{1,0:T(2,128)(2,1)}, u32[]{:S(2)}) copy-start(bf16[2,448]{1,0:T(2,128)(2,1)} %param.27) | copy-start | bytes 5380
  509.1 30.5 %copy-start.43 = (f32[2,448]{1,0:T(2,128)S(1)}, f32[2,448]{1,0:T(2,128)}, u32[]{:S(2)}) copy-start(f32[2,448]{1,0:T(2,128)} %param.41) | copy-start | bytes 10756
  509.2 30.5 %copy-start.44 = (f32[2,448]{1,0:T(2,128)S(1)}, f32[2,448]{1,0:T(2,128)}, u32[]{:S(2)}) copy-start(f32[2,448]{1,0:T(2,128)} %param.34) | copy-start | bytes 10756
  509.2 31.1 %copy-start.32 = (f32[4,448]{1,0:T(4,128)S(1)}, f32[4,448]{1,0:T(4,128)}, u32[]{:S(2)}) copy-start(f32[4,448]{1,0:T(4,128)} %param.44) | copy-start | bytes 21508
  509.2 31.1 %copy-start.33 = (f32[4,448]{1,0:T(4,128)S(1)}, f32[4,448]{1,0:T(4,128)}, u32[]{:S(2)}) copy-start(f32[4,448]{1,0:T(4,128)} %param.37) | copy-start | bytes 21508
  539.6 91.1 %copy-start.34 = (f32[4,448]{1,0:T(4,128)}, f32[4,448]{1,0:T(4,128)S(1)}, u32[]{:S(2)}) copy-start(f32[4,448]{1,0:T(4,128)S(1)} %get-tuple-element.187) | copy-start | bytes 21508
  539.6 91.1 %copy-start.45 = (f32[2,448]{1,0:T(2,128)}, f32[2,448]{1,0:T(2,128)S(1)}, u32[]{:S(2)}) copy-start(f32[2,448]{1,0:T(2,128)S(1)} %get-tuple-element.186) | copy-start | bytes 10756
  (26 other events, 50.4 us)
Sparse Core Ops, SparseCore 0:
  57.4 86.3 all-reduce.15
  159.7 131.4 all-gather.3
  294.1 23.3 reduce-scatter.18
  321.3 65.8 reduce-scatter.16
  390.9 35.3 reduce-scatter.20
  429.1 77.6 all-reduce.17
  510.2 47.6 reduce-scatter.22
  561.3 66.8 reduce-scatter.12
  631.7 102.3 reduce-scatter.14
